TPU v7x, 32 devices: a whole 2x2x4 slice. The times are simulated.
32 devices in a mesh: section: 2 (over core), dp: 8 (over z, x), rep: 2 (over y).
Axes of the slice: x: 2, y: 2, z: 4, core: 2. Of those that a mesh axis runs over, the one named last changes fastest.
Arguments:
- inputs: bfloat16 [4096, 1024], P(('dp', 'rep')), may hold values from -6 to 6
- cotangent: bfloat16 [4096, 1024], P(('dp', 'rep')), may hold values from -6 to 6
- seg_counts: int32 [256], P(('dp', 'rep')), may hold values from 2 to 16
- w_qkv: bfloat16 [2, 1024, 3072], P('section'), may hold values from -0.1875 to 0.1875
- w_out: bfloat16 [2, 1024, 1024], P('section'), may hold values from -0.375 to 0.375
- w_up: bfloat16 [2, 1024, 2048], P('section'), may hold values from -0.1875 to 0.1875
- w_down: bfloat16 [2, 2048, 1024], P('section'), may hold values from -0.1875 to 0.1875
- gains: float32 [2, 2, 1024], P('section'), may hold values from 0.5 to 1.5
- biases: float32 [2, 2, 1024], P('section'), may hold values from -3 to 3
Outputs:
- layer_outputs: bfloat16 [2, 4096, 1024], P('section', ('dp', 'rep'))
- input_grads: bfloat16 [2, 4096, 1024], P('section', ('dp', 'rep'))
- grad_qkv: float32 [2, 1024, 3072], P('section', 'dp')
- grad_wout: float32 [2, 1024, 1024], P('section', None, 'dp')
- grad_up: float32 [2, 1024, 2048], P('section', 'dp')
- grad_down: float32 [2, 2048, 1024], P('section', None, 'dp')
- grad_gains: float32 [2, 2, 1024], P('section', None, 'dp')
- grad_biases: float32 [2, 2, 1024], P('section', None, 'dp')
Inputs may be any that keep to these rules, and one draw needn't show every extreme that they name: seg_counts gives each series' number of valid slots; the first 16 - seg_counts slots of a series are padding.
All inputs are finite; a program needn't handle non-finite values.
Results may differ from a plain program's by a relative error of at most 0.015.
Values may be sent and summed in bfloat16 or wider, within the bound.
A program may use at most 256 MiB of HBM per device.

v0:
```python
from functools import partial
import jax
import jax.numpy as jnp
from jax import lax
from jax.sharding import PartitionSpec as P

SEG = 16
HEAD_DIM = 128
BLOCK = 128
epsilon = 1e-05
f32 = jnp.float32
bf16 = jnp.bfloat16


def normalize(hidden):
    average = jnp.mean(hidden, axis=-1, keepdims=True)
    centred = hidden - average
    inverse = lax.rsqrt(jnp.mean(centred * centred, axis=-1, keepdims=True) + epsilon)
    return (centred * inverse, inverse)


def normalize_back(grad_normed, normed, inverse):
    centre_term = jnp.mean(grad_normed, axis=-1, keepdims=True)
    slope_term = normed * jnp.mean(grad_normed * normed, axis=-1, keepdims=True)
    return inverse * (grad_normed - centre_term - slope_term)


def allowed_pairs(counts):
    rows = counts.shape[0] * SEG
    blocks = rows // BLOCK
    ids = jnp.arange(rows, dtype=jnp.int32).reshape(blocks, BLOCK)
    first = jnp.repeat(SEG - counts, SEG).reshape(blocks, BLOCK)
    position = ids % SEG
    owner = ids // SEG
    same = owner[:, :, None] == owner[:, None, :]
    causal = position[:, None, :] <= position[:, :, None]
    valid = (position >= first)[:, None, :] | (ids[:, :, None] == ids[:, None, :])
    return same & causal & valid


def forward(hidden_b, params, allowed):
    w_qkv, w_out, w_up, w_down, gains, biases = params
    rows = hidden_b.shape[0]
    heads = w_qkv.shape[1] // (3 * HEAD_DIM)
    hidden = hidden_b.astype(f32)
    n1, i1 = normalize(hidden)
    a = (n1 * gains[0] + biases[0]).astype(bf16)
    packed = jnp.dot(a, w_qkv, preferred_element_type=f32).astype(bf16)
    split = packed.reshape(rows // BLOCK, BLOCK, 3, heads, HEAD_DIM)
    scores = jnp.einsum(
        "bqhd,bkhd->bhqk", split[:, :, 0], split[:, :, 1], preferred_element_type=f32
    )
    scores = jnp.where(allowed[:, None], scores * HEAD_DIM ** (-0.5), -1e30)
    raised = jnp.exp(scores - jnp.max(scores, axis=-1, keepdims=True))
    probs = raised / jnp.sum(raised, axis=-1, keepdims=True)
    probs_b = probs.astype(bf16)
    mixed = jnp.einsum("bhqk,bkhd->bqhd", probs_b, split[:, :, 2], preferred_element_type=f32)
    mixed_b = mixed.reshape(rows, heads * HEAD_DIM).astype(bf16)
    middle = hidden + jnp.dot(mixed_b, w_out, preferred_element_type=f32)
    n2, i2 = normalize(middle)
    c = (n2 * gains[1] + biases[1]).astype(bf16)
    upper = jnp.dot(c, w_up, preferred_element_type=f32)
    g = jax.nn.gelu(upper, approximate=True).astype(bf16)
    result = (middle + jnp.dot(g, w_down, preferred_element_type=f32)).astype(bf16)
    return (result, (n1, i1, a, split, probs, probs_b, mixed_b, n2, i2, c, upper, g))


def backward(saved, grad_b, params):
    w_qkv, w_out, w_up, w_down, gains, biases = params
    n1, i1, a, split, probs, probs_b, mixed_b, n2, i2, c, upper, g = saved
    rows = grad_b.shape[0]
    heads = w_qkv.shape[1] // (3 * HEAD_DIM)
    d_g = jnp.einsum("rd,fd->rf", grad_b, w_down, preferred_element_type=f32)
    d_u = jax.vjp(partial(jax.nn.gelu, approximate=True), upper)[1](d_g)[0].astype(bf16)
    d_c = jnp.einsum("rf,df->rd", d_u, w_up, preferred_element_type=f32)
    d_m = grad_b.astype(f32) + normalize_back(d_c * gains[1], n2, i2)
    d_mb = d_m.astype(bf16)
    d_o = jnp.einsum("ro,io->ri", d_mb, w_out, preferred_element_type=f32).astype(bf16)
    d_o = d_o.reshape(rows // BLOCK, BLOCK, heads, HEAD_DIM)
    d_probs = jnp.einsum("bqhd,bkhd->bhqk", d_o, split[:, :, 2], preferred_element_type=f32)
    d_v = jnp.einsum("bhqk,bqhd->bkhd", probs_b, d_o, preferred_element_type=f32)
    d_s = (probs * (d_probs - jnp.sum(probs * d_probs, axis=-1, keepdims=True))).astype(bf16)
    d_q = jnp.einsum(
        "bhqk,bkhd->bqhd", d_s, split[:, :, 1], preferred_element_type=f32
    ) * HEAD_DIM ** (-0.5)
    d_k = jnp.einsum(
        "bhqk,bqhd->bkhd", d_s, split[:, :, 0], preferred_element_type=f32
    ) * HEAD_DIM ** (-0.5)
    d_p = jnp.stack((d_q, d_k, d_v), axis=2).reshape(rows, -1).astype(bf16)
    d_a = jnp.einsum("re,de->rd", d_p, w_qkv, preferred_element_type=f32)
    d_h = (d_m + normalize_back(d_a * gains[0], n1, i1)).astype(bf16)
    return (d_h, (d_u, d_mb, d_p, d_a, d_c))


def per_device(inputs, cotangent, seg_counts, w_qkv, w_out, w_up, w_down, gains, biases):
    last = lax.axis_size("section") - 1
    section = lax.axis_index("section")
    params = (w_qkv[0], w_out[0], w_up[0], w_down[0], gains[0], biases[0])
    allowed = allowed_pairs(seg_counts)
    sent = forward(inputs, params, allowed)[0]
    hidden = jnp.where(section == 0, inputs, lax.ppermute(sent, "section", [(0, 1)]))
    result, saved = forward(hidden, params, allowed)
    sent = backward(saved, cotangent, params)[0]
    grad = jnp.where(section == last, cotangent, lax.ppermute(sent, "section", [(1, 0)]))
    d_h, (d_u, d_mb, d_p, d_a, d_c) = backward(saved, grad, params)
    n1, i1, a, split, probs, probs_b, mixed_b, n2, i2, c, upper, g = saved

    def outer(left, right):
        return jnp.einsum("ri,ro->io", left, right, preferred_element_type=f32).astype(bf16)[None]

    terms = (outer(a, d_p), outer(mixed_b, d_mb), outer(c, d_u), outer(g, grad))
    small_g = jnp.stack((jnp.sum(d_a * n1, axis=0), jnp.sum(d_c * n2, axis=0)))[None]
    small_b = jnp.stack((jnp.sum(d_a, axis=0), jnp.sum(d_c, axis=0)))[None]
    terms = terms + (small_g, small_b)
    dims = (1, 2, 1, 2, 2, 2)
    shares = [
        lax.psum_scatter(term, "dp", scatter_dimension=dim, tiled=True)
        for term, dim in zip(terms, dims)
    ]
    summed = [lax.psum(share.astype(bf16), "rep").astype(f32) for share in shares]
    return (result[None], d_h[None], *summed)


def solution(mesh):
    rows = P(("dp", "rep"), None)
    layer = P("section", None, None)
    return jax.shard_map(
        per_device,
        mesh=mesh,
        in_specs=(rows, rows, P(("dp", "rep"))) + (layer,) * 6,
        out_specs=(
            P("section", ("dp", "rep"), None),
            P("section", ("dp", "rep"), None),
            P("section", "dp", None),
            P("section", None, "dp"),
            P("section", "dp", None),
            P("section", None, "dp"),
            P("section", None, "dp"),
            P("section", None, "dp"),
        ),
        check_vma=False,
    )
```

profile of v0, /device:TPU:0, one launch (start us, length us, event | category | flops | bytes accessed | tf_op | source)
XLA Modules:
  0.0 717.0 jit_solution(17454511011516978575)
XLA Ops:
  12.4 4.9 fusion.63
  20.2 2.9 fusion.125
  26.4 7.5 %fusion.93 = bf16[256,1024]{1,0:T(8,128)(2,1)} fusion(f32[256,1024]{1,0:T(8,128)} %copy-done.15, bf16[1,2048,1024]{2,1,0:T(8,128)(2,1)} %param.15, bf16[1,1024,2048]{2,1,0:T(8,128)(2,1)} %param.14, f32[1024]{0:T(1024)S(1)} %bitcast.290, f32[1024]{0:T(1024)S(1)} %bitcast.281, f32[256]{0:T(256)S(1)} %add_rsqrt_fusion.2, f32[256]{0:T(256)S(1)} %broadcast_multiply_fusion.10), kind=kOutput, calls=%fused_computation.92 | convolution fusion | flops 2154037248 | bytes 9971712 | tf_op jit(solution)/shard_map/dot_general | solution.py:64
  38.5 4.7 fusion.60
  55.6 2.7 fusion.22
  58.3 8.4 %fusion.198 = (f32[256]{0:T(256)S(1)}, f32[256]{0:T(256)S(1)}, f32[256,1024]{1,0:T(8,128)}) fusion(f32[256]{0:T(256)S(1)} %add_rsqrt_fusion, f32[256,1024]{1,0:T(8,128)S(1)} %get-tuple-element.43, f32[256]{0:T(256)S(1)} %broadcast_multiply_fusion.8, f32[1024]{0:T(1024)S(1)} %bitcast.283, bf16[1,1024,2048]{2,1,0:T(8,128)(2,1)} %param.14, ...), kind=kOutput, calls=%fused_computation.231 | convolution fusion | flops 2159541760 | bytes 13115392 | tf_op jit(solution)/shard_map/rf,df->rd/dot_general | solution.py:75
  72.0 3.0 fusion.127
  79.1 11.6 %pad_maximum_fusion = bf16[2,128,3,8,128]{4,1,3,0,2:T(8,128)(2,1)S(1)} fusion(bf16[2,128,1,8,128]{4,1,3,0,2:T(8,128)(2,1)S(1)} %copy-done.25, bf16[2,128,1,8,128]{4,1,3,0,2:T(8,128)(2,1)S(1)} %fusion.114, bf16[2,128,1,8,128]{4,1,3,0,2:T(8,128)(2,1)S(1)} %fusion.115), kind=kLoop, calls=%fused_computation.63 | loop fusion | flops 1572864 | bytes 3145728 | tf_op jit(solution)/shard_map/stack | solution.py:89
  92.8 3.7 convert_element_type.182
  96.6 5.4 fusion.197
  104.8 2.8 collective-permute-done.1
  108.8 5.4 add_convert_fusion
  119.6 10.8 %copy.135 = bf16[1,1024,1024]{1,0,2:T(2,128)(2,1)} copy(bf16[1,1024,1024]{2,1,0:T(8,128)(2,1)} %convert_bitcast_fusion.3) | data formatting | bytes 4194304
  130.5 4.3 copy.188
  134.8 5.3 convert_bitcast_fusion.1
  140.1 20.6 %copy.137 = bf16[1,2048,1024]{1,0,2:T(2,128)(2,1)} copy(bf16[1,2048,1024]{2,1,0:T(8,128)(2,1)} %convert_bitcast_fusion.1) | data formatting | bytes 8388608
  160.7 8.0 %copy.187 = bf16[1024,1,2048]{2,0,1:T(8,128)(2,1)} copy(bf16[1024,1,2048]{2,1,0:T(2,128)(2,1)} %bitcast.260) | data formatting | bytes 8388608
  168.8 5.0 convert_bitcast_fusion.2
  177.8 3.1 convolution_bitcast_fusion
  187.4 3.7 convert_element_type.190
  191.1 6.2 convert_bitcast_fusion
  197.4 6.4 fusion.140
  209.9 85.5 %reduce-scatter.21.cloned.1.call-done = bf16[128,2048]{1,0:T(8,128)(2,1)} async-done(((bf16[1024,2048]{1,0:T(8,128)(2,1)}), bf16[128,2048]{1,0:T(8,128)(2,1)}) %reduce-scatter.21.cloned.1.call-update) | async-done | bytes 524304
  295.4 2.6 reshape_bitcast_fusion
  298.1 3.5 copy.138
  301.6 85.6 %reduce-scatter.17.cloned.1.call-done = bf16[1,128,2048]{2,1,0:T(8,128)(2,1)} async-done(((bf16[1,1024,2048]{2,1,0:T(8,128)(2,1)}), bf16[1,128,2048]{2,1,0:T(8,128)(2,1)}) %reduce-scatter.17.cloned.1.call-update) | async-done | bytes 524304 | tf_op jit(solution)/shard_map/reduce_scatter | solution.py:117
  387.2 121.2 %reduce-scatter.15.cloned.1.call-done = bf16[1,128,3072]{2,1,0:T(8,128)(2,1)} async-done(((bf16[1,1024,3072]{2,1,0:T(8,128)(2,1)}), bf16[1,128,3072]{2,1,0:T(8,128)(2,1)}) %reduce-scatter.15.cloned.1.call-update) | async-done | bytes 786448 | tf_op jit(solution)/shard_map/reduce_scatter | solution.py:117
  508.5 5.5 fusion.122
  515.2 57.5 %reduce-scatter.25.cloned.1.call-done = f32[128,2]{1,0:T(8,128)} async-done(((f32[1024,2]{1,0:T(8,128)}), f32[128,2]{1,0:T(8,128)}) %reduce-scatter.25.cloned.1.call-update) | async-done | bytes 1040
  573.6 64.2 %reduce-scatter.23.cloned.1.call-done = f32[128,2]{1,0:T(8,128)} async-done(((f32[1024,2]{1,0:T(8,128)}), f32[128,2]{1,0:T(8,128)}) %reduce-scatter.23.cloned.1.call-update) | async-done | bytes 1040
  638.7 4.9 all-reduce
  644.7 58.6 %all-reduce.4.cloned.1.call-done = (bf16[1,128,3072]{2,1,0:T(8,128)(2,1)}, bf16[1,1024,128]{2,1,0:T(8,128)(2,1)}, bf16[1,128,2048]{2,1,0:T(8,128)(2,1)}, bf16[1,2048,128]{2,1,0:T(8,128)(2,1)}) async-done(((bf16[1,128,3072]{2,1,0:T(8,128)(2,1)}, bf16[1,1024,128]{2,1,0:T(8,128)(2,1)}, bf16[1,128,2048]{2,1,0:T(8,128)(2,1)}, bf16[1,2048,128]{2,1,0:T(8,128)(2,1)}), (bf16[1,128,3072]{2,1,0:T(8,128)(2,1)}, ...) | async-done | bytes 2097168 | tf_op jit(solution)/shard_map/psum | solution.py:120
  (160 shorter events, 76.3 us)
Async XLA Ops:
  7.2 17.2 %copy-start = (bf16[1,1024,1024]{2,1,0:T(8,128)(2,1)S(1)}, bf16[1,1024,1024]{2,1,0:T(8,128)(2,1)}, u32[]{:S(2)}) copy-start(bf16[1,1024,1024]{2,1,0:T(8,128)(2,1)} %param.13) | copy-start | bytes 6291460
  7.2 198.8 %reduce-scatter.19.cloned.1.call-start = ((), (), s32[]{:S(2)}) async-start(), calls=%async_computation.8 | async-start | bytes 2359296
  20.2 4.2 copy-start.7
  33.9 4.1 collective-permute-start
  38.2 5.1 copy-start.2
  44.7 5.1 copy-start.9
  44.7 5.1 copy-start.12
  53.1 2.5 copy-start.26
  55.2 59.0 %copy-start.1 = (f32[256,1024]{1,0:T(8,128)}, f32[256,1024]{1,0:T(8,128)S(1)}, u32[]{:S(2)}) copy-start(f32[256,1024]{1,0:T(8,128)S(1)} %get-tuple-element.43) | copy-start | bytes 3145732
  74.9 2.0 copy-start.5
  77.0 1.3 copy-start.13
  78.0 1.1 copy-start.25
  96.6 5.5 copy-start.3
  96.6 5.5 copy-start.16
  96.6 5.5 copy-start.21
  103.5 4.1 collective-permute-start.1
  108.8 7.1 copy-start.17
  108.8 5.4 copy-start.27
  114.2 1.6 copy-start.28
  115.8 1.7 copy-start.8
  134.8 160.7 %reduce-scatter.21.cloned.1.call-start = ((), (), s32[]{:S(2)}) async-start(), calls=%async_computation.9 | async-start | bytes 4718592
  168.8 218.4 %reduce-scatter.17.cloned.1.call-start = ((), (), s32[]{:S(2)}) async-start(), calls=%async_computation.7 | async-start | bytes 4718592 | tf_op jit(solution)/shard_map/reduce_scatter | solution.py:117
  173.8 334.6 %reduce-scatter.15.cloned.1.call-start = ((), (), s32[]{:S(2)}) async-start(), calls=%async_computation.6 | async-start | bytes 7077888 | tf_op jit(solution)/shard_map/reduce_scatter | solution.py:117
  180.9 2.0 copy-start.6
  182.9 1.4 copy-start.11
  197.3 375.4 %reduce-scatter.25.cloned.1.call-start = ((), (), s32[]{:S(2)}) async-start(), calls=%async_computation.11 | async-start | bytes 589824
  204.8 432.9 %reduce-scatter.23.cloned.1.call-start = ((), (), s32[]{:S(2)}) async-start(), calls=%async_computation.10 | async-start | bytes 589824
  206.0 497.3 %all-reduce.4.cloned.1.call-start = ((), (), s32[]{:S(2)}) async-start(), calls=%async_computation.12 | async-start | bytes 4194304 | tf_op jit(solution)/shard_map/psum | solution.py:120
  508.4 5.5 copy-start.4
  508.4 5.5 copy-start.18
  703.3 4.3 copy-start.23
  705.1 3.6 copy-start.22
  (6 other events, 6.1 us)
Sparse Core Ops, SparseCore 0:
  134.9 69.7 reduce-scatter.18
  208.3 87.0 reduce-scatter.20
  299.5 87.6 reduce-scatter.16
  390.6 117.7 reduce-scatter.14
  511.6 61.0 reduce-scatter.24
  576.8 60.8 reduce-scatter.22
  640.8 62.4 all-reduce.3
where the time goes:
time: 725 us; the launch traced here: 717 us
  waiting for transfers between devices  477 us (66%)
  matrix products  94.3 us (13%)
  local copies, waits for them, and re-layouts  90 us (12%)
  other arithmetic  31.2 us (4%)
  between operations  15.1 us (2%)
    unnamed x11, waiting for transfers between devices  207 us
    reduce_scatter x2, waiting for transfers between devices, per_device(): lax.psum_scatter(term, 'dp', scatter_dimension=dim, tiled=True)  207 us
    unnamed x76, local copies, waits for them, and re-layouts  68.5 us
    psum x1, waiting for transfers between devices, per_device(): lax.psum(share.astype(bf16), 'rep').astype(f32)  58.6 us
    dot_general x4, matrix products, outer(): jnp.einsum('ri,ro->io', left, right, preferred_element_type=f32)  18.5 us
  transfers between devices with their start and end apart: 9, of which 8 were waited for; matrix products, arithmetic and copies ran while one was open for 12% of the time, Pallas kernels for 0%

commit v1 on v0

--- a/solution.py
+++ b/solution.py
@@ -10,6 +10,7 @@
 epsilon = 1e-05
 f32 = jnp.float32
 bf16 = jnp.bfloat16
+cubes_direct = lambda x_local: jnp.sum(lax.all_gather(x_local, axis_name="rep"), axis=0)
 
 
 def normalize(hidden):
@@ -117,7 +118,7 @@
         lax.psum_scatter(term, "dp", scatter_dimension=dim, tiled=True)
         for term, dim in zip(terms, dims)
     ]
-    summed = [lax.psum(share.astype(bf16), "rep").astype(f32) for share in shares]
+    summed = [cubes_direct(share.astype(bf16)).astype(f32) for share in shares]
     return (result[None], d_h[None], *summed)
 
 

time: 725 us -> 702 us (0.968)
  waiting for transfers between devices: 477 us -> 451 us
  blocking collectives: 4.94 us -> 15.5 us
  other arithmetic: 31.2 us -> 22.9 us
    reduce_scatter x2, waiting for transfers between devices: 207 us -> 111 us  [per_device(): lax.psum_scatter(term, 'dp', scatter_dimension=dim, tiled=True)]
    unnamed x11 -> x13, waiting for transfers between devices: 207 us -> 277 us
    all_gather x0 -> x3, waiting for transfers between devices: none -> 59.1 us  [lax.all_gather(x_local, axis_name='rep')]
    psum x1 -> x0, waiting for transfers between devices: 58.6 us -> none  [per_device(): lax.psum(share.astype(bf16), 'rep').astype(f32)]
    all_gather x0 -> x3, blocking collectives: none -> 15.5 us  [lax.all_gather(x_local, axis_name='rep')]
    another operation x1, other arithmetic: 11.6 us -> 0.38 us  [backward(): d_p = jnp.stack((d_q, d_k, d_v), axis=2).reshape(rows, -1).astype(bf16)]
    unnamed x76 -> x70, local copies, waits for them, and re-layouts: 68.5 us -> 67.5 us
  transfers between devices with their start and end apart: 9 -> 11, of which waited for: 8 -> 10; matrix products, arithmetic and copies ran while one was open for 12% -> 16% of each run, Pallas kernels for 0% -> 0%
where the time goes in v1:
time: 702 us; the launch traced here: 694 us
  waiting for transfers between devices  451 us (64%)
  matrix products  96.1 us (14%)
  local copies, waits for them, and re-layouts  89.1 us (13%)
  other arithmetic  22.9 us (3%)
  blocking collectives  15.5 us (2%)
  between operations  14.6 us (2%)
    unnamed x13, waiting for transfers between devices  277 us
    reduce_scatter x2, waiting for transfers between devices, per_device(): lax.psum_scatter(term, 'dp', scatter_dimension=dim, tiled=True)  111 us
    unnamed x70, local copies, waits for them, and re-layouts  67.5 us
    all_gather x3, waiting for transfers between devices, lax.all_gather(x_local, axis_name='rep')  59.1 us
    dot_general x4, matrix products, outer(): jnp.einsum('ri,ro->io', left, right, preferred_element_type=f32)  18 us
    all_gather x3, blocking collectives, lax.all_gather(x_local, axis_name='rep')  15.5 us
  transfers between devices with their start and end apart: 11, of which 10 were waited for; matrix products, arithmetic and copies ran while one was open for 16% of the time, Pallas kernels for 0%

profile of v1, /device:TPU:0, one launch (start us, length us, event | category | flops | bytes accessed | tf_op | source)
XLA Modules:
  0.0 693.7 jit_solution(1856469828723809944)
XLA Ops:
  12.4 4.9 fusion.63
  26.4 7.5 %fusion.93 = bf16[256,1024]{1,0:T(8,128)(2,1)} fusion(f32[256,1024]{1,0:T(8,128)} %copy-done.14, bf16[1,2048,1024]{2,1,0:T(8,128)(2,1)} %param.15, bf16[1,1024,2048]{2,1,0:T(8,128)(2,1)} %param.14, f32[1024]{0:T(1024)S(1)} %bitcast.308, f32[1024]{0:T(1024)S(1)} %bitcast.299, f32[256]{0:T(256)S(1)} %add_rsqrt_fusion.2, f32[256]{0:T(256)S(1)} %broadcast_multiply_fusion.10), kind=kOutput, calls=%fused_computation.92 | convolution fusion | flops 2154037248 | bytes 9971712 | tf_op jit(solution)/shard_map/dot_general | solution.py:65
  38.5 4.7 fusion.60
  58.2 8.4 %fusion.198 = (f32[256]{0:T(256)S(1)}, f32[256]{0:T(256)S(1)}, f32[256,1024]{1,0:T(8,128)}) fusion(f32[256]{0:T(256)S(1)} %add_rsqrt_fusion, f32[256,1024]{1,0:T(8,128)S(1)} %get-tuple-element.37, f32[256]{0:T(256)S(1)} %broadcast_multiply_fusion.8, f32[1024]{0:T(1024)S(1)} %bitcast.301, bf16[1,1024,2048]{2,1,0:T(8,128)(2,1)} %param.14, ...), kind=kOutput, calls=%fused_computation.237 | convolution fusion | flops 2159541760 | bytes 13115392 | tf_op jit(solution)/shard_map/rf,df->rd/dot_general | solution.py:76
  81.5 3.7 convert_element_type.260
  85.3 5.4 fusion.197
  97.5 5.3 add_convert_fusion
  103.8 3.4 convert_bitcast_fusion.2
  107.3 5.3 convert_bitcast_fusion.1
  112.5 20.6 %copy.137 = bf16[1,2048,1024]{1,0,2:T(2,128)(2,1)} copy(bf16[1,2048,1024]{2,1,0:T(8,128)(2,1)} %convert_bitcast_fusion.1) | data formatting | bytes 8388608
  133.2 8.2 %copy.187 = bf16[1024,1,2048]{2,0,1:T(8,128)(2,1)} copy(bf16[1024,1,2048]{2,1,0:T(2,128)(2,1)} %bitcast.278) | data formatting | bytes 8388608
  141.8 4.2 multiply_reduce_fusion
  151.5 3.0 convolution_bitcast_fusion
  160.9 3.7 convert_element_type.268
  164.7 6.3 fusion.140
  173.2 6.2 convert_bitcast_fusion
  179.7 3.1 convert_bitcast_fusion.3
  182.9 10.9 %copy.135 = bf16[1,1024,1024]{1,0,2:T(2,128)(2,1)} copy(bf16[1,1024,1024]{2,1,0:T(8,128)(2,1)} %convert_bitcast_fusion.3) | data formatting | bytes 4194304
  193.8 4.4 copy.188
  199.0 90.5 %reduce-scatter.21.cloned.1.call-done = bf16[128,2048]{1,0:T(8,128)(2,1)} async-done(((bf16[1024,2048]{1,0:T(8,128)(2,1)}), bf16[128,2048]{1,0:T(8,128)(2,1)}) %reduce-scatter.21.cloned.1.call-update) | async-done | bytes 524304
  292.1 3.5 copy.138
  295.7 5.5 fusion.122
  302.4 52.1 %reduce-scatter.25.cloned.1.call-done = f32[128,2]{1,0:T(8,128)} async-done(((f32[1024,2]{1,0:T(8,128)}), f32[128,2]{1,0:T(8,128)}) %reduce-scatter.25.cloned.1.call-update) | async-done | bytes 1040
  355.4 63.5 %reduce-scatter.23.cloned.1.call-done = f32[128,2]{1,0:T(8,128)} async-done(((f32[1024,2]{1,0:T(8,128)}), f32[128,2]{1,0:T(8,128)}) %reduce-scatter.23.cloned.1.call-update) | async-done | bytes 1040
  419.8 4.2 all-gather.5
  424.0 4.2 all-gather.4
  428.8 110.6 %reduce-scatter.15.cloned.1.call-done = bf16[1,128,3072]{2,1,0:T(8,128)(2,1)} async-done(((bf16[1,1024,3072]{2,1,0:T(8,128)(2,1)}), bf16[1,128,3072]{2,1,0:T(8,128)(2,1)}) %reduce-scatter.15.cloned.1.call-update) | async-done | bytes 786448 | tf_op jit(solution)/shard_map/reduce_scatter | solution.py:118
  540.0 69.8 %reduce-scatter.19.cloned.1.call-done = bf16[128,1024]{1,0:T(8,128)(2,1)} async-done(((bf16[1024,1024]{1,0:T(8,128)(2,1)}), bf16[128,1024]{1,0:T(8,128)(2,1)}) %reduce-scatter.19.cloned.1.call-update) | async-done | bytes 262160
  611.5 7.0 %all-gather.1 = bf16[2,1024,128]{2,1,0:T(8,128)(2,1)S(1)} all-gather(bf16[1,1024,128]{2,1,0:T(8,128)(2,1)S(1)} %copy.136), channel_id=3, replica_groups=mesh['section'=2,'dp'=8,'rep'=2] {'rep'}, dimensions={0}, use_global_device_ids=true | all-gather | bytes 786432 | tf_op jit(solution)/shard_map/all_gather | solution.py:13
  619.6 12.1 %all-gather.12.cloned.1.call-done = bf16[2,128,2048]{2,1,0:T(8,128)(2,1)} async-done(((bf16[1,128,2048]{2,1,0:T(8,128)(2,1)}), bf16[2,128,2048]{2,1,0:T(8,128)(2,1)}) %all-gather.12.cloned.1.call-update) | async-done | bytes 1048592 | tf_op jit(solution)/shard_map/all_gather | solution.py:13
  633.1 22.0 %all-gather.14.cloned.1.call-done = bf16[2,2048,128]{2,1,0:T(8,128)(2,1)} async-done(((bf16[1,2048,128]{2,1,0:T(8,128)(2,1)}), bf16[2,2048,128]{2,1,0:T(8,128)(2,1)}) %all-gather.14.cloned.1.call-update) | async-done | bytes 1048592 | tf_op jit(solution)/shard_map/all_gather | solution.py:13
  659.0 25.0 %all-gather.10.cloned.1.call-done = bf16[2,128,3072]{2,1,0:T(8,128)(2,1)} async-done(((bf16[1,128,3072]{2,1,0:T(8,128)(2,1)}), bf16[2,128,3072]{2,1,0:T(8,128)(2,1)}) %all-gather.10.cloned.1.call-update) | async-done | bytes 1572880 | tf_op jit(solution)/shard_map/all_gather | solution.py:13
  (168 shorter events, 89.7 us)
Async XLA Ops:
  7.2 17.2 %copy-start = (bf16[1,1024,1024]{2,1,0:T(8,128)(2,1)S(1)}, bf16[1,1024,1024]{2,1,0:T(8,128)(2,1)}, u32[]{:S(2)}) copy-start(bf16[1,1024,1024]{2,1,0:T(8,128)(2,1)} %param.13) | copy-start | bytes 6291460
  7.2 191.0 %reduce-scatter.17.cloned.1.call-start = ((), (), s32[]{:S(2)}) async-start(), calls=%async_computation.7 | async-start | bytes 4718592 | tf_op jit(solution)/shard_map/reduce_scatter | solution.py:118
  20.2 4.2 copy-start.7
  33.9 4.1 collective-permute-start
  38.2 5.1 copy-start.2
  44.7 5.1 copy-start.8
  44.7 5.1 copy-start.11
  53.0 2.5 copy-start.24
  55.2 86.6 %copy-start.1 = (f32[256,1024]{1,0:T(8,128)}, f32[256,1024]{1,0:T(8,128)S(1)}, u32[]{:S(2)}) copy-start(f32[256,1024]{1,0:T(8,128)S(1)} %get-tuple-element.37) | copy-start | bytes 3145732
  74.9 2.0 copy-start.5
  76.9 1.3 copy-start.12
  77.9 1.1 copy-start.23
  85.2 5.5 copy-start.3
  85.3 5.5 copy-start.15
  85.3 5.5 copy-start.21
  92.2 4.1 collective-permute-start.1
  97.5 5.4 copy-start.16
  107.2 182.2 %reduce-scatter.21.cloned.1.call-start = ((), (), s32[]{:S(2)}) async-start(), calls=%async_computation.12 | async-start | bytes 4718592
  141.4 213.1 %reduce-scatter.25.cloned.1.call-start = ((), (), s32[]{:S(2)}) async-start(), calls=%async_computation.14 | async-start | bytes 589824
  141.8 4.2 copy-start.17
  154.5 2.0 copy-start.6
  156.5 1.0 copy-start.13
  156.5 1.4 copy-start.10
  157.5 1.1 copy-start.22
  172.0 246.9 %reduce-scatter.23.cloned.1.call-start = ((), (), s32[]{:S(2)}) async-start(), calls=%async_computation.13 | async-start | bytes 589824
  173.2 366.2 %reduce-scatter.15.cloned.1.call-start = ((), (), s32[]{:S(2)}) async-start(), calls=%async_computation.6 | async-start | bytes 7077888 | tf_op jit(solution)/shard_map/reduce_scatter | solution.py:118
  179.5 430.3 %reduce-scatter.19.cloned.1.call-start = ((), (), s32[]{:S(2)}) async-start(), calls=%async_computation.11 | async-start | bytes 2359296
  198.2 433.5 %all-gather.12.cloned.1.call-start = ((), (), s32[]{:S(2)}) async-start(), calls=%async_computation.9 | async-start | bytes 1572864 | tf_op jit(solution)/shard_map/all_gather | solution.py:13
  198.9 456.2 %all-gather.14.cloned.1.call-start = ((), (), s32[]{:S(2)}) async-start(), calls=%async_computation.10 | async-start | bytes 1572864 | tf_op jit(solution)/shard_map/all_gather | solution.py:13
  295.6 388.3 %all-gather.10.cloned.1.call-start = ((), (), s32[]{:S(2)}) async-start(), calls=%async_computation.8 | async-start | bytes 2359296 | tf_op jit(solution)/shard_map/all_gather | solution.py:13
  295.7 5.5 copy-start.4
  295.7 5.5 copy-start.18
  (5 other events, 4.9 us)
Sparse Core Ops, SparseCore 0:
  107.3 90.1 reduce-scatter.16
  201.5 87.8 reduce-scatter.20
  292.8 61.6 reduce-scatter.24
  358.0 60.8 reduce-scatter.22
  422.3 117.0 reduce-scatter.14
  542.8 66.9 reduce-scatter.18
  611.4 20.2 all-gather.11
  633.8 21.2 all-gather.13
  656.7 27.2 all-gather.9
